TPU v7x, 32 devices: a whole 2x2x4 slice. The times are simulated.
32 devices in a mesh: fields: 2 (over x), prow: 8 (over z, y), pcol: 2 (over core).
Axes of the slice: x: 2, y: 2, z: 4, core: 2. Of those that a mesh axis runs over, the one named last changes fastest.
Arguments:
- inverse_tiles: bfloat16 [32, 16, 256, 256], P(('fields', 'prow'), 'pcol'), parts along dimension 0, may hold values from -6 to 6
- panel_blocks: bfloat16 [4, 8, 256, 512], P('fields', 'prow', None, 'pcol'), parts along dimension 0, may hold values from -0.125 to 0.125
- diag_inverse: float32 [4, 512], P('fields', 'pcol'), parts along dimension 0, may hold values from 0.5 to 2
- structure: int32 [4, 8], P('fields'), parts along dimension 0, may hold values from 0 to 15, as said below
- block_slot: int32 [32], P('fields'), parts along dimension 0, may hold values from 0 to 15, each once
Outputs:
- sigma_new: bfloat16 [4, 16, 256, 512], P('fields', 'prow', None, 'pcol'), parts along dimension 0
- variances: float32 [4, 512], P('fields', 'pcol'), parts along dimension 0
There are 2 independent parts, one for each index of `fields`. A program takes and returns all parts, laid end to end along the dimension named above; each array names one. Nothing has to cross between parts.
Inputs may be any that keep to these rules, and one draw needn't show every extreme that they name: `structure`: each row lists 8 distinct row blocks in increasing order, and the last is always 16 - 1. `block_slot`: each slot is used by exactly one row block.
All inputs are finite; a program needn't handle non-finite values.
Results may differ from a plain program's by a relative error of at most 0.0006.
Values may be sent and summed in bfloat16 or wider, within the bound.
No kernel may reach another device: no remote copies, remote signals or barrier semaphores. Data moves between devices by JAX's collectives and lax.ppermute only.
A program may use at most 128 MiB of HBM per device.

v0:
```python
import jax
import jax.numpy as jnp
from jax import lax
from jax.sharding import PartitionSpec as P


def swapped(shard, axis, stride):
    return lax.ppermute(shard, axis, [(i, i ^ 1 << stride) for i in range(lax.axis_size(axis))])


def make_accumulate(selected, row_hits, piece):
    contrib = jnp.einsum("iskxy,skyw->sixw", selected, piece, preferred_element_type=jnp.float32)
    own_panel = jnp.einsum("sik,skxw->sixw", row_hits, piece, preferred_element_type=jnp.float32)
    return (contrib, own_panel)


def per_device(inverse_tiles, panel_blocks, diag_inverse, structure, block_slot):
    rows_here = inverse_tiles.shape[0]
    tile_size = inverse_tiles.shape[2]
    supernodes = panel_blocks.shape[0]
    positions = structure.shape[1]
    prow_index = lax.axis_index("prow")
    pcol_index = lax.axis_index("pcol")
    slot_of = block_slot[structure]
    own_rows = prow_index * rows_here + jnp.arange(rows_here, dtype=jnp.int32)
    row_match = slot_of[:, None, :] == own_rows[None, :, None]
    row_hits = row_match.astype(jnp.bfloat16)
    row_used = jnp.any(row_match, axis=2)
    partner = swapped(inverse_tiles, "pcol", 0)
    first_half = jnp.where(pcol_index == 0, inverse_tiles, partner)
    second_half = jnp.where(pcol_index == 0, partner, inverse_tiles)
    whole_rows = jnp.concatenate([first_half, second_half], axis=1)
    selected = jnp.take(whole_rows, slot_of.reshape(-1), axis=1)
    selected = selected.reshape(rows_here, supernodes, positions, tile_size, tile_size)
    summed, own_panel = make_accumulate(
        selected, row_hits, lax.all_gather(panel_blocks, "prow", axis=1, tiled=True)
    )
    sigma_rows = jnp.where(row_used[:, :, None, None], -summed, jnp.zeros((), jnp.float32))
    partial_value = jnp.sum(own_panel * sigma_rows, axis=(1, 2))
    correction = lax.psum(partial_value, "prow")
    variances = diag_inverse - correction
    return (sigma_rows.astype(jnp.bfloat16), variances)


def solution(mesh):
    in_specs = (
        P(("fields", "prow"), "pcol", None, None),
        P("fields", "prow", None, "pcol"),
        P("fields", "pcol"),
        P("fields", None),
        P("fields"),
    )
    out_specs = (P("fields", "prow", None, "pcol"), P("fields", "pcol"))
    return jax.shard_map(
        per_device, mesh=mesh, in_specs=in_specs, out_specs=out_specs, check_vma=False
    )
```

profile of v0, /device:TPU:0, one launch (start us, length us, event | category | flops | bytes accessed | tf_op | source)
XLA Modules:
  0.0 95.9 jit_solution(17099047433927221169)
XLA Ops:
  7.2 0.0 copy-start
  7.2 0.0 all-gather.2.cloned.1.call-start
  7.2 0.7 all-gather.2.cloned.1.call-update
  7.9 0.6 collective-permute-start
  8.5 0.7 compare_select_fusion.1
  9.2 0.1 reshape.53
  9.2 0.0 copy-done
  9.2 0.7 gather_fusion
  9.9 0.1 reshape.52
  10.0 0.2 compare_reduce_fusion
  10.2 2.3 %collective-permute-done = bf16[2,8,256,256]{3,2,1,0:T(8,128)(2,1)S(1)} collective-permute-done((bf16[2,8,256,256]{3,2,1,0:T(8,128)(2,1)}, bf16[2,8,256,256]{3,2,1,0:T(8,128)(2,1)S(1)}, u32[]{:S(2)}, u32[]{:S(2)}) %collective-permute-start) | collective-permute-done | bytes 2097184 | tf_op jit(solution)/shard_map/ppermute | solution.py:8
  12.5 1.9 %broadcast_select_fusion.1 = (bf16[2,8,256,256]{3,2,1,0:T(8,128)(2,1)S(1)}, bf16[2,8,256,256]{3,2,1,0:T(8,128)(2,1)S(1)}) fusion(bf16[2,8,256,256]{3,2,1,0:T(8,128)(2,1)} %param.5, bf16[2,8,256,256]{3,2,1,0:T(8,128)(2,1)S(1)} %collective-permute-done, pred[]{:T(512)S(6)} %eq.20), kind=kLoop, calls=%fused_computation.11 | loop fusion | flops 2097152 | bytes 8388609 | tf_op jit(solution)/shard_map/jit(_where)/select_n | solution.py:30
  14.3 2.3 %pad_maximum_fusion = bf16[2,16,256,256]{3,2,1,0:T(8,128)(2,1)} fusion(bf16[2,8,256,256]{3,2,1,0:T(8,128)(2,1)S(1)} %get-tuple-element.3, bf16[2,8,256,256]{3,2,1,0:T(8,128)(2,1)S(1)} %get-tuple-element.2), kind=kLoop, calls=%fused_computation.2 | loop fusion | flops 2097152 | bytes 8388608 | tf_op jit(solution)/shard_map/concatenate | solution.py:32
  16.7 4.9 %gather_fusion.1 = bf16[16,2,256,256]{3,2,1,0:T(8,128)(2,1)} fusion(bf16[2,16,256,256]{3,2,1,0:T(8,128)(2,1)} %pad_maximum_fusion, s32[1024]{0:T(1024)S(1)} %pad_clamp_fusion), kind=kCustom, calls=%fused_computation.1 | custom fusion | bytes 8388672 | tf_op jit(solution)/shard_map/jit(_take)/gather | solution.py:33
  21.6 40.4 %all-gather.2.cloned.1.call-done = bf16[2,8,256,256]{3,2,1,0:T(8,128)(2,1)} async-done(((bf16[2,1,256,256]{3,2,1,0:T(8,128)(2,1)}), bf16[2,8,256,256]{3,2,1,0:T(8,128)(2,1)}) %all-gather.2.cloned.1.call-update) | async-done | bytes 2097168 | tf_op jit(solution)/shard_map/all_gather | solution.py:36
  62.0 0.0 copy-start.1
  62.0 3.2 %fusion.3 = f32[2,2,256,256]{3,1,2,0:T(2,128)S(1)} fusion(bf16[2,8,256,256]{3,2,1,0:T(8,128)(2,1)} %all-gather.2.cloned.1.call-done, s32[2,8]{1,0:T(2,128)S(1)} %reshape.52, s32[2]{0:T(128)S(1)} %iota_add_fusion), kind=kOutput, calls=%fused_computation.7 | convolution fusion | flops 4194336 | bytes 3145800 | tf_op jit(solution)/shard_map/sik,skxw->sixw/dot_general | solution.py:13
  65.2 0.0 copy-done.1
  65.2 0.0 copy-start.2
  65.2 4.3 %fusion.15 = (f32[2,256]{1,0:T(2,128)S(1)}, bf16[2,2,256,256]{3,2,1,0:T(8,128)(2,1)}) fusion(f32[2,2,256,256]{3,1,2,0:T(2,128)S(1)} %fusion.3, bf16[2,8,256,256]{3,2,1,0:T(8,128)(2,1)S(1)} %copy-done.1, bf16[2,2,8,256,256]{4,3,0,2,1:T(8,128)(2,1)} %bitcast.32, pred[2,8]{1,0:T(4,128)(4,1)S(1)} %compare_and_fusion, pred[2,2]{1,0:T(4,128)(4,1)S(1)} %compare_reduce_fusion), kind=kOutput, calls=%fused_computation.16 | convolution fusion | flops 1077149184 | bytes 7866388 | tf_op jit(solution)/shard_map/iskxy,skyw->sixw/dot_general | solution.py:12
  69.5 19.0 %psum.7 = f32[2,256]{1,0:T(2,128)S(1)} all-reduce(f32[2,256]{1,0:T(2,128)S(1)} %get-tuple-element.4), channel_id=1, replica_groups=mesh['fields'=2,'prow'=8,'pcol'=2] {'prow'}, use_global_device_ids=true, to_apply=%region_2.3 | all-reduce | flops 512 | bytes 4096 | tf_op jit(solution)/shard_map/psum | solution.py:40
  88.5 0.0 copy-done.2
  88.5 0.6 sub.3
  (5 shorter events, 0.0 us)
Async XLA Ops:
  7.2 2.1 %copy-start = (s32[16]{0:T(128)S(1)}, s32[16]{0:T(128)}, u32[]{:S(2)}) copy-start(s32[16]{0:T(128)} %param.9) | copy-start | bytes 196
  7.2 54.8 %all-gather.2.cloned.1.call-start = ((), (), s32[]{:S(2)}) async-start(), calls=%async_computation | async-start | bytes 2359296 | tf_op jit(solution)/shard_map/all_gather | solution.py:36
  7.9 4.6 %collective-permute-start = (bf16[2,8,256,256]{3,2,1,0:T(8,128)(2,1)}, bf16[2,8,256,256]{3,2,1,0:T(8,128)(2,1)S(1)}, u32[]{:S(2)}, u32[]{:S(2)}) collective-permute-start(bf16[2,8,256,256]{3,2,1,0:T(8,128)(2,1)} %param.5), channel_id=1, source_target_pairs={{0,1},{1,0},{2,3},{3,2},{4,5},{5,4},{6,7},{7,6},{8,9},{9,8},{10,11... | collective-permute-start | bytes 6291464 | tf_op jit(solution)/shard_map/ppermute | solution.py:8
  62.0 3.2 %copy-start.1 = (bf16[2,8,256,256]{3,2,1,0:T(8,128)(2,1)S(1)}, bf16[2,8,256,256]{3,2,1,0:T(8,128)(2,1)}, u32[]{:S(2)}) copy-start(bf16[2,8,256,256]{3,2,1,0:T(8,128)(2,1)} %all-gather.2.cloned.1.call-done) | copy-start | bytes 6291460
  65.2 23.3 %copy-start.2 = (f32[2,256]{1,0:T(2,128)S(1)}, f32[2,256]{1,0:T(2,128)}, u32[]{:S(2)}) copy-start(f32[2,256]{1,0:T(2,128)} %param.7) | copy-start | bytes 6148
Sparse Core Ops, SparseCore 0:
  10.2 51.7 all-gather.1
where the time goes:
time: 96.1 us; the launch traced here: 95.9 us
  waiting for transfers between devices  43.3 us (45%)
  blocking collectives  19 us (20%)
  between operations  14.1 us (15%)
  matrix products  7.51 us (8%)
  local copies, waits for them, and re-layouts  5.78 us (6%)
  other arithmetic  5.67 us (6%)
    all_gather x1, waiting for transfers between devices, per_device(): lax.all_gather(panel_blocks, 'prow', axis=1, tiled=True)  40.4 us
    psum x1, blocking collectives, per_device(): correction = lax.psum(partial_value, 'prow')  19 us
    gather x1, local copies, waits for them, and re-layouts, per_device(): selected = jnp.take(whole_rows, slot_of.reshape(-1), axis=1)  4.94 us
    dot_general x1, matrix products, make_accumulate(): jnp.einsum('iskxy,skyw->sixw', selected, piece, preferred_element_type=jn...  4.32 us
    dot_general x1, matrix products, make_accumulate(): jnp.einsum('sik,skxw->sixw', row_hits, piece, preferred_element_type=jnp....  3.19 us
    concatenate x1, other arithmetic, per_device(): whole_rows = jnp.concatenate([first_half, second_half], axis=1)  2.33 us
    ppermute x1, waiting for transfers between devices, swapped(): lax.ppermute(shard, axis, [(i, i ^ 1 << stride) for i in range(lax.axis_s...  2.26 us
  transfers between devices with their start and end apart: 2, of which 2 were waited for; matrix products, arithmetic and copies ran while one was open for 11% of the time, Pallas kernels for 0%

commit v1 on v0

--- a/solution.py
+++ b/solution.py
@@ -37,7 +37,7 @@
     )
     sigma_rows = jnp.where(row_used[:, :, None, None], -summed, jnp.zeros((), jnp.float32))
     partial_value = jnp.sum(own_panel * sigma_rows, axis=(1, 2))
-    correction = lax.psum(partial_value, "prow")
+    correction = jnp.sum(lax.all_gather(partial_value, "prow"), axis=0)
     variances = diag_inverse - correction
     return (sigma_rows.astype(jnp.bfloat16), variances)
 

time: 96.1 us -> 103 us (1.072)
  blocking collectives: 19 us -> 26.1 us
    all_gather x0 -> x1, blocking collectives: none -> 26.1 us  [per_device(): correction = jnp.sum(lax.all_gather(partial_value, 'prow'), axis=0)]
    psum x1 -> x0, blocking collectives: 19 us -> none  [per_device(): correction = lax.psum(partial_value, 'prow')]
where the time goes in v1:
time: 103 us
  waiting for transfers between devices  43.3 us (42%)
  blocking collectives  26.1 us (25%)
  between operations  14.1 us (14%)
  matrix products  7.51 us (7%)
  local copies, waits for them, and re-layouts  5.78 us (6%)
  other arithmetic  5.69 us (6%)
    all_gather x1, waiting for transfers between devices, per_device(): lax.all_gather(panel_blocks, 'prow', axis=1, tiled=True)  40.4 us
    all_gather x1, blocking collectives, per_device(): correction = jnp.sum(lax.all_gather(partial_value, 'prow'), axis=0)  26.1 us
    gather x1, local copies, waits for them, and re-layouts, per_device(): selected = jnp.take(whole_rows, slot_of.reshape(-1), axis=1)  4.94 us
    dot_general x1, matrix products, make_accumulate(): jnp.einsum('iskxy,skyw->sixw', selected, piece, preferred_element_type=jn...  4.32 us
    dot_general x1, matrix products, make_accumulate(): jnp.einsum('sik,skxw->sixw', row_hits, piece, preferred_element_type=jnp....  3.19 us
    concatenate x1, other arithmetic, per_device(): whole_rows = jnp.concatenate([first_half, second_half], axis=1)  2.33 us
    ppermute x1, waiting for transfers between devices, swapped(): lax.ppermute(shard, axis, [(i, i ^ 1 << stride) for i in range(lax.axis_s...  2.26 us
  transfers between devices with their start and end apart: 2, of which 2 were waited for; matrix products, arithmetic and copies ran while one was open for 11% of the time, Pallas kernels for 0%

profile of v1, /device:TPU:0, one launch (start us, length us, event | category | flops | bytes accessed | tf_op | source)
XLA Modules:
  0.0 103.1 jit_solution(17944252983502595990)
XLA Ops:
  7.2 0.0 copy-start
  7.2 0.0 all-gather.4.cloned.1.call-start
  7.2 0.7 all-gather.4.cloned.1.call-update
  7.9 0.6 collective-permute-start
  8.5 0.7 compare_select_fusion.1
  9.2 0.1 reshape.53
  9.2 0.0 copy-done
  9.2 0.7 gather_fusion
  9.9 0.1 reshape.52
  10.0 0.2 compare_reduce_fusion
  10.2 2.3 %collective-permute-done = bf16[2,8,256,256]{3,2,1,0:T(8,128)(2,1)S(1)} collective-permute-done((bf16[2,8,256,256]{3,2,1,0:T(8,128)(2,1)}, bf16[2,8,256,256]{3,2,1,0:T(8,128)(2,1)S(1)}, u32[]{:S(2)}, u32[]{:S(2)}) %collective-permute-start) | collective-permute-done | bytes 2097184 | tf_op jit(solution)/shard_map/ppermute | solution.py:8
  12.5 1.9 %broadcast_select_fusion.1 = (bf16[2,8,256,256]{3,2,1,0:T(8,128)(2,1)S(1)}, bf16[2,8,256,256]{3,2,1,0:T(8,128)(2,1)S(1)}) fusion(bf16[2,8,256,256]{3,2,1,0:T(8,128)(2,1)} %param.5, bf16[2,8,256,256]{3,2,1,0:T(8,128)(2,1)S(1)} %collective-permute-done, pred[]{:T(512)S(6)} %eq.20), kind=kLoop, calls=%fused_computation.11 | loop fusion | flops 2097152 | bytes 8388609 | tf_op jit(solution)/shard_map/jit(_where)/select_n | solution.py:30
  14.3 2.3 %pad_maximum_fusion = bf16[2,16,256,256]{3,2,1,0:T(8,128)(2,1)} fusion(bf16[2,8,256,256]{3,2,1,0:T(8,128)(2,1)S(1)} %get-tuple-element.3, bf16[2,8,256,256]{3,2,1,0:T(8,128)(2,1)S(1)} %get-tuple-element.2), kind=kLoop, calls=%fused_computation.2 | loop fusion | flops 2097152 | bytes 8388608 | tf_op jit(solution)/shard_map/concatenate | solution.py:32
  16.7 4.9 %gather_fusion.1 = bf16[16,2,256,256]{3,2,1,0:T(8,128)(2,1)} fusion(bf16[2,16,256,256]{3,2,1,0:T(8,128)(2,1)} %pad_maximum_fusion, s32[1024]{0:T(1024)S(1)} %pad_clamp_fusion), kind=kCustom, calls=%fused_computation.1 | custom fusion | bytes 8388672 | tf_op jit(solution)/shard_map/jit(_take)/gather | solution.py:33
  21.6 40.4 %all-gather.4.cloned.1.call-done = bf16[2,8,256,256]{3,2,1,0:T(8,128)(2,1)} async-done(((bf16[2,1,256,256]{3,2,1,0:T(8,128)(2,1)}), bf16[2,8,256,256]{3,2,1,0:T(8,128)(2,1)}) %all-gather.4.cloned.1.call-update) | async-done | bytes 2097168 | tf_op jit(solution)/shard_map/all_gather | solution.py:36
  62.0 0.0 copy-start.1
  62.0 3.2 %fusion.3 = f32[2,2,256,256]{3,1,2,0:T(2,128)S(1)} fusion(bf16[2,8,256,256]{3,2,1,0:T(8,128)(2,1)} %all-gather.4.cloned.1.call-done, s32[2,8]{1,0:T(2,128)S(1)} %reshape.52, s32[2]{0:T(128)S(1)} %iota_add_fusion), kind=kOutput, calls=%fused_computation.7 | convolution fusion | flops 4194336 | bytes 3145800 | tf_op jit(solution)/shard_map/sik,skxw->sixw/dot_general | solution.py:13
  65.2 0.0 copy-done.1
  65.2 0.0 copy-start.2
  65.2 4.3 %fusion.15 = (f32[2,256]{1,0:T(2,128)S(1)}, bf16[2,2,256,256]{3,2,1,0:T(8,128)(2,1)}) fusion(f32[2,2,256,256]{3,1,2,0:T(2,128)S(1)} %fusion.3, bf16[2,8,256,256]{3,2,1,0:T(8,128)(2,1)S(1)} %copy-done.1, bf16[2,2,8,256,256]{4,3,0,2,1:T(8,128)(2,1)} %bitcast.33, pred[2,8]{1,0:T(4,128)(4,1)S(1)} %compare_and_fusion, pred[2,2]{1,0:T(4,128)(4,1)S(1)} %compare_reduce_fusion), kind=kOutput, calls=%fused_computation.16 | convolution fusion | flops 1077149184 | bytes 7866388 | tf_op jit(solution)/shard_map/iskxy,skyw->sixw/dot_general | solution.py:12
  69.5 26.1 %all-gather.1 = f32[8,2,256]{2,1,0:T(2,128)S(1)} all-gather(f32[1,2,256]{2,1,0:T(2,128)S(1)} %bitcast.34), channel_id=2, replica_groups=mesh['fields'=2,'prow'=8,'pcol'=2] {'prow'}, dimensions={0}, use_global_device_ids=true | all-gather | bytes 18432 | tf_op jit(solution)/shard_map/all_gather | solution.py:40
  95.6 0.0 copy-done.2
  95.7 0.6 sub.3
  (6 shorter events, 0.1 us)
Async XLA Ops:
  7.2 2.1 %copy-start = (s32[16]{0:T(128)S(1)}, s32[16]{0:T(128)}, u32[]{:S(2)}) copy-start(s32[16]{0:T(128)} %param.9) | copy-start | bytes 196
  7.2 54.8 %all-gather.4.cloned.1.call-start = ((), (), s32[]{:S(2)}) async-start(), calls=%async_computation | async-start | bytes 2359296 | tf_op jit(solution)/shard_map/all_gather | solution.py:36
  7.9 4.6 %collective-permute-start = (bf16[2,8,256,256]{3,2,1,0:T(8,128)(2,1)}, bf16[2,8,256,256]{3,2,1,0:T(8,128)(2,1)S(1)}, u32[]{:S(2)}, u32[]{:S(2)}) collective-permute-start(bf16[2,8,256,256]{3,2,1,0:T(8,128)(2,1)} %param.5), channel_id=1, source_target_pairs={{0,1},{1,0},{2,3},{3,2},{4,5},{5,4},{6,7},{7,6},{8,9},{9,8},{10,11... | collective-permute-start | bytes 6291464 | tf_op jit(solution)/shard_map/ppermute | solution.py:8
  62.0 3.2 %copy-start.1 = (bf16[2,8,256,256]{3,2,1,0:T(8,128)(2,1)S(1)}, bf16[2,8,256,256]{3,2,1,0:T(8,128)(2,1)}, u32[]{:S(2)}) copy-start(bf16[2,8,256,256]{3,2,1,0:T(8,128)(2,1)} %all-gather.4.cloned.1.call-done) | copy-start | bytes 6291460
  65.2 30.5 %copy-start.2 = (f32[2,256]{1,0:T(2,128)S(1)}, f32[2,256]{1,0:T(2,128)}, u32[]{:S(2)}) copy-start(f32[2,256]{1,0:T(2,128)} %param.7) | copy-start | bytes 6148
Sparse Core Ops, SparseCore 0:
  10.2 51.7 all-gather.3
